TPU v7x, 32 devices: a whole 2x2x4 slice. The times are simulated.
32 devices in a mesh: row: 4 (over y, core), col: 8 (over z, x).
Axes of the slice: x: 2, y: 2, z: 4, core: 2. Of those that a mesh axis runs over, the one named last changes fastest.
Arguments:
- normal: float32 [16, 4, 256, 8, 8, 256], P(None, 'row', None, None, 'col'), may hold values from -1.5 to 1.5
- panel_inverse: float32 [256, 256], replicated, as said below
- rhs: float32 [16, 4, 256, 512], P(None, 'row', None, 'col'), may hold values from -0.009765625 to 0.009765625
- shifts: float32 [4], replicated, may hold values from 16 to 128
Outputs:
- schur: float32 [16, 4, 256, 8, 8, 256], P(None, 'row', None, None, 'col')
- eliminated: float32 [16, 4, 256, 512], P(None, 'row', None, 'col')
- applied: float32 [16, 4, 256, 512], P(None, 'row', None, 'col')
Inputs may be any that keep to these rules, and one draw needn't show every extreme that they name: `panel_inverse`: lower triangular with positive diagonal entries.
All inputs are finite; a program needn't handle non-finite values.
Results may differ from a plain program's by a relative error of at most 0.000076.
Values sent between devices are 32-bit elements; how exact they have to be, the bound alone decides.
A program may use at most 256 MiB of HBM per device.

v0:
```python
import jax
import jax.numpy as jnp
from jax import lax
from jax.sharding import PartitionSpec as P

R = 128


def spread_2(value, axis, source):
    kept = jnp.where(lax.axis_index(axis) == source, value, 0).astype(value.dtype)
    return lax.psum(kept, axis)


def pick_blocks(blocks, spacing, offset):
    grouped = blocks.reshape((blocks.shape[0] // spacing, spacing) + blocks.shape[1:])
    return lax.dynamic_index_in_dim(grouped, offset, 1, keepdims=False)


def shards(normal, panel_inverse, rhs, shifts):
    high = lax.Precision.HIGHEST
    row_index = lax.axis_index("row")
    col_index = lax.axis_index("col")
    nrow = lax.axis_size("row")
    ncol = lax.axis_size("col")
    spacing = ncol // nrow
    brows, nb, bcols = (normal.shape[0], normal.shape[2], normal.shape[3])
    narrow = rhs.shape[3]
    wide = narrow * ncol
    tile = normal.reshape(brows * nb, bcols * nb)
    owner = col_index % nrow
    offset = col_index // nrow
    local_panel = jnp.dot(
        tile[:, :nb], panel_inverse.T, precision=high, preferred_element_type=jnp.float32
    )
    panel = spread_2(local_panel, "col", 0)
    chosen = pick_blocks(panel.reshape(brows, nb, nb), spacing, offset)
    crossed = spread_2(chosen, "row", owner).reshape(bcols * nb, nb)
    updated = tile - jnp.dot(panel, crossed.T, precision=high, preferred_element_type=jnp.float32)
    leading = spread_2(rhs[0, 0], "row", 0)
    first = jnp.dot(panel_inverse, leading, precision=high, preferred_element_type=jnp.float32)
    reduced = rhs.reshape(brows * nb, narrow) - jnp.dot(
        panel, first, precision=high, preferred_element_type=jnp.float32
    )
    reduced = reduced.reshape(brows, nb, narrow)
    reduced = reduced.at[0].set(jnp.where(row_index == 0, first, reduced[0]))
    spread = lax.all_gather(reduced, "col", axis=2, tiled=True)
    scales = lax.dynamic_slice_in_dim(jnp.repeat(shifts, R), col_index * narrow, narrow)
    partial_value = lax.dot_general(
        updated,
        spread.reshape(brows * nb, wide),
        (((0,), (0,)), ((), ())),
        precision=high,
        preferred_element_type=jnp.float32,
    )
    totals = lax.psum(partial_value, "row")
    totals = totals.reshape(bcols, nb, ncol, narrow)
    arrived = lax.all_to_all(totals, "col", split_axis=2, concat_axis=2, tiled=True)
    arrived = arrived.reshape(bcols, nb, spacing, nrow, narrow)
    arrived = lax.dynamic_index_in_dim(arrived, row_index, 3, keepdims=False)
    product = jnp.transpose(arrived, (0, 2, 1, 3)).reshape(brows, nb, narrow)
    applied = product + reduced * scales[None, None, :]
    schur = updated.reshape(brows, 1, nb, bcols, 1, nb)
    return (schur, reduced.reshape(brows, 1, nb, narrow), applied.reshape(brows, 1, nb, narrow))


def solution(mesh):
    in_specs = (P(None, "row", None, None, "col", None), P(), P(None, "row", None, "col"), P())
    out_specs = (
        P(None, "row", None, None, "col", None),
        P(None, "row", None, "col"),
        P(None, "row", None, "col"),
    )
    return jax.shard_map(shards, mesh=mesh, in_specs=in_specs, out_specs=out_specs, check_vma=False)
```

profile of v0, /device:TPU:0, one launch (start us, length us, event | category | flops | bytes accessed | tf_op | source)
XLA Modules:
  0.0 758.9 jit_solution(6350466244515718778)
XLA Ops:
  7.2 93.9 %reduce.2 = f32[16,256,8,256]{3,2,1,0:T(8,128)} reduce(f32[16,1,256,8,1,256]{5,4,3,2,1,0:T(1,128)} %param.6, f32[]{:T(128)} %constant.77), dimensions={1,4}, to_apply=%param.6.reduce_sub_computation | reduce | bytes 67108864 | tf_op args[0]
  101.1 29.9 %copy.37 = f32[512,8,8,256]{3,1,2,0:T(8,128)} copy(f32[512,8,8,256]{3,2,1,0:T(8,128)} %bitcast.49) | data formatting | bytes 67108864
  131.1 7.7 %convolution_select_fusion = f32[4096,256]{1,0:T(8,128)} fusion(f32[256,256]{1,0:T(8,128)S(1)} %copy-done, f32[4096,2048]{1,0:T(8,128)} %bitcast.47, pred[]{:T(512)S(6)} %eq.12), kind=kOutput, calls=%fused_computation.1 | convolution fusion | flops 3222274048 | bytes 8650753 | tf_op jit(solution)/shard_map/dot_general | solution.py:32
  138.8 1.1 copy-done.5
  140.6 157.4 %all-reduce.5.cloned.1.call-done = f32[4096,256]{1,0:T(8,128)} async-done(((f32[4096,256]{1,0:T(8,128)}), f32[4096,256]{1,0:T(8,128)}) %all-reduce.5.cloned.1.call-update) | async-done | bytes 4194320 | tf_op jit(solution)/shard_map/psum | solution.py:11
  298.0 3.1 dynamic-slice_select_fusion
  301.7 51.0 %all-reduce.9.cloned.1.call-done = (f32[2048,256]{1,0:T(8,128)}, f32[256,64]{0,1:T(8,128)}) async-done(((f32[2048,256]{1,0:T(8,128)}, f32[256,64]{0,1:T(8,128)}), (f32[2048,256]{1,0:T(8,128)}, f32[256,64]{0,1:T(8,128)})) %all-reduce.9.cloned.1.call-update) | async-done | bytes 2162704 | tf_op jit(solution)/shard_map/psum | solution.py:11
  352.7 1.2 fusion.3
  354.0 6.5 convolution_subtract_fusion.1
  360.9 0.9 scatter.4
  361.8 1.0 copy-done.2
  362.9 34.1 %convolution_subtract_fusion = f32[4096,2048]{1,0:T(8,128)} fusion(f32[4096,2048]{1,0:T(8,128)} %bitcast.48, f32[4096,256]{1,0:T(8,128)} %all-reduce.5.cloned.1.call-done, f32[2048,256]{1,0:T(8,128)S(1)} %copy-done.4), kind=kOutput, calls=%fused_computation | convolution fusion | flops 25778192384 | bytes 73400320 | tf_op jit(solution)/shard_map/dot_general | solution.py:38
  397.0 90.5 %all-gather.2.cloned.1.call-done = f32[16,256,512]{1,0,2:T(8,128)} async-done(((f32[16,256,64]{1,0,2:T(8,128)}), f32[16,256,512]{1,0,2:T(8,128)}) %all-gather.2.cloned.1.call-update) | async-done | bytes 8388624 | tf_op jit(solution)/shard_map/all_gather | solution.py:46
  487.5 9.9 %copy.28 = f32[16,256,512]{2,1,0:T(8,128)} copy(f32[16,256,512]{1,0,2:T(8,128)} %all-gather.2.cloned.1.call-done) | data formatting | bytes 16777216 | tf_op jit(solution)/shard_map/all_gather | solution.py:46
  497.4 64.5 %fusion.4 = f32[2048,512]{0,1:T(8,128)S(1)} fusion(f32[4096,2048]{1,0:T(8,128)} %convolution_subtract_fusion, f32[4096,512]{1,0:T(8,128)} %bitcast.55), kind=kOutput, calls=%fused_computation.13 | convolution fusion | flops 51539607552 | bytes 46137344 | tf_op jit(solution)/shard_map/dot_general | solution.py:48
  561.9 4.0 copy.40
  565.9 83.8 %all-reduce.7.cloned.1.call-done = f32[8,256,8,64]{1,0,3,2:T(8,128)} async-done(((f32[8,256,8,64]{1,0,3,2:T(8,128)}), f32[8,256,8,64]{1,0,3,2:T(8,128)}) %all-reduce.7.cloned.1.call-update) | async-done | bytes 4194320 | tf_op jit(solution)/shard_map/psum | solution.py:55
  649.7 5.5 all-to-all-start
  655.4 48.4 %reshape.98 = f32[16,1,256,8,1,256]{5,4,3,2,1,0:T(1,128)} reshape(f32[4096,2048]{1,0:T(8,128)} %convolution_subtract_fusion) | data formatting | bytes 67108864 | tf_op jit(solution)/shard_map/reshape | solution.py:62
  703.8 1.6 copy.33
  705.4 42.8 %all-to-all-done = f32[8,256,8,64]{1,0,3,2:T(8,128)} async-done(((f32[8,256,8,64]{1,0,3,2:T(8,128)}), f32[8,256,8,64]{1,0,3,2:T(8,128)}, u32[]{:S(2)}, u32[]{:S(2)}) %all-to-all-start) | async-done | bytes 4194336 | tf_op jit(solution)/shard_map/all_to_all | solution.py:57
  748.2 1.3 constant_dynamic-slice_fusion
  749.9 0.7 fusion.1
  750.6 1.6 copy.34
  (28 shorter events, 2.3 us)
Async XLA Ops:
  7.2 123.9 %copy-start = (f32[256,256]{1,0:T(8,128)S(1)}, f32[256,256]{1,0:T(8,128)}, u32[]{:S(2)}) copy-start(f32[256,256]{1,0:T(8,128)} %param.7) | copy-start | bytes 786436
  7.2 290.8 %all-reduce.5.cloned.1.call-start = ((), (), s32[]{:S(2)}) async-start(), calls=%async_computation.1 | async-start | bytes 8388608 | tf_op jit(solution)/shard_map/psum | solution.py:11
  138.7 1.2 copy-start.5
  138.7 214.0 %all-reduce.9.cloned.1.call-start = ((), (), s32[]{:S(2)}) async-start(), calls=%async_computation.4 | async-start | bytes 4325376 | tf_op jit(solution)/shard_map/psum | solution.py:11
  301.1 186.4 %all-gather.2.cloned.1.call-start = ((), (), s32[]{:S(2)}) async-start(), calls=%async_computation.2 | async-start | bytes 9437184 | tf_op jit(solution)/shard_map/all_gather | solution.py:46
  354.0 8.9 %copy-start.4 = (f32[2048,256]{1,0:T(8,128)S(1)}, f32[2048,256]{1,0:T(8,128)}, u32[]{:S(2)}) copy-start(f32[2048,256]{1,0:T(8,128)} %get-tuple-element.27) | copy-start | bytes 6291460
  361.8 1.0 copy-start.2
  362.8 286.9 %all-reduce.7.cloned.1.call-start = ((), (), s32[]{:S(2)}) async-start(), calls=%async_computation.3 | async-start | bytes 8388608 | tf_op jit(solution)/shard_map/psum | solution.py:55
  565.9 89.3 %copy-start.6 = (f32[4]{0:T(128)S(1)}, f32[4]{0:T(128)}, u32[]{:S(2)}) copy-start(f32[4]{0:T(128)} %param.9) | copy-start | bytes 52
  649.7 98.5 %all-to-all-start = ((f32[8,256,8,64]{1,0,3,2:T(8,128)}), f32[8,256,8,64]{1,0,3,2:T(8,128)}, u32[]{:S(2)}, u32[]{:S(2)}) async-start(f32[8,256,8,64]{1,0,3,2:T(8,128)} %all-reduce.7.cloned.1.call-done), calls=%async_computation | async-start | bytes 8388608 | tf_op jit(solution)/shard_map/all_to_all | solution.py:57
  655.4 48.4 %copy-start.3 = (f32[16,256,64]{1,0,2:T(8,128)S(1)}, f32[16,256,64]{1,0,2:T(8,128)}, u32[]{:S(2)}) copy-start(f32[16,256,64]{1,0,2:T(8,128)} %copy-done.2) | copy-start | bytes 3145732
  748.2 3.9 copy-start.1
Sparse Core Ops, SparseCore 0:
  138.9 159.0 all-reduce.4
  301.2 51.4 all-reduce.8
  362.9 124.5 all-gather.1
  566.0 83.6 all-reduce.6
where the time goes:
time: 768 us; the launch traced here: 759 us
  waiting for transfers between devices  426 us (55%)
  matrix products  114 us (15%)
  local copies, waits for them, and re-layouts  101 us (13%)
  other arithmetic  98.3 us (13%)
  between operations  14.1 us (2%)
    psum x2, waiting for transfers between devices, spread_2(): return lax.psum(kept, axis)  208 us
    unnamed x1, other arithmetic  93.9 us
    all_gather x1, waiting for transfers between devices, shards(): spread = lax.all_gather(reduced, 'col', axis=2, tiled=True)  90.5 us
    psum x1, waiting for transfers between devices, shards(): totals = lax.psum(partial_value, 'row')  83.8 us
    dot_general x1, matrix products, shards(): lax.dot_general(updated, spread.reshape(brows * nb, wide), (((0,), (0,)),...  64.5 us
    reshape x1, local copies, waits for them, and re-layouts, shards(): schur = updated.reshape(brows, 1, nb, bcols, 1, nb)  48.4 us
    all_to_all x1, waiting for transfers between devices, shards(): lax.all_to_all(totals, 'col', split_axis=2, concat_axis=2, tiled=True)  42.8 us
    unnamed x21, local copies, waits for them, and re-layouts  39.9 us
  transfers between devices with their start and end apart: 5, of which 5 were waited for; matrix products, arithmetic and copies ran while one was open for 11% of the time, Pallas kernels for 0%

commit v1 on v0

--- a/solution.py
+++ b/solution.py
@@ -43,7 +43,12 @@
     )
     reduced = reduced.reshape(brows, nb, narrow)
     reduced = reduced.at[0].set(jnp.where(row_index == 0, first, reduced[0]))
-    spread = lax.all_gather(reduced, "col", axis=2, tiled=True)
+    ring = [reduced]
+    for hop in range(7):
+        ring.append(lax.ppermute(ring[-1], "col", [(dev, (dev + 1) % 8) for dev in range(8)]))
+    spread = jnp.roll(
+        jnp.concatenate(ring[::-1], axis=2), (lax.axis_index("col") + 1) * ring[0].shape[2], axis=2
+    )
     scales = lax.dynamic_slice_in_dim(jnp.repeat(shifts, R), col_index * narrow, narrow)
     partial_value = lax.dot_general(
         updated,

time: 768 us -> 879 us (1.14)
  waiting for transfers between devices: 426 us -> 490 us
  local copies, waits for them, and re-layouts: 101 us -> 147 us
    ppermute x0 -> x7, waiting for transfers between devices: none -> 150 us  [shards(): lax.ppermute(ring[-1], 'col', [(dev, (dev + 1) % 8) for dev in range(8)])]
    all_gather x1 -> x0, waiting for transfers between devices: 90.5 us -> none  [shards(): spread = lax.all_gather(reduced, 'col', axis=2, tiled=True)]
    concatenate x0 -> x1, local copies, waits for them, and re-layouts: none -> 24.4 us  [shards(): jnp.roll(jnp.concatenate(ring[::-1], axis=2), (lax.axis_index('col') + 1)...]
    ppermute x0 -> x7, local copies, waits for them, and re-layouts: none -> 19.9 us  [shards(): lax.ppermute(ring[-1], 'col', [(dev, (dev + 1) % 8) for dev in range(8)])]
    all_gather x1 -> x0, local copies, waits for them, and re-layouts: 9.9 us -> none  [shards(): spread = lax.all_gather(reduced, 'col', axis=2, tiled=True)]
  transfers between devices with their start and end apart: 5 -> 11, of which waited for: 5 -> 10; matrix products, arithmetic and copies ran while one was open for 11% -> 12% of each run, Pallas kernels for 0% -> 0%
where the time goes in v1:
time: 879 us; the launch traced here: 869 us
  waiting for transfers between devices  490 us (56%)
  local copies, waits for them, and re-layouts  147 us (17%)
  matrix products  110 us (13%)
  other arithmetic  101 us (11%)
  between operations  14.1 us (2%)
    psum x2, waiting for transfers between devices, spread_2(): return lax.psum(kept, axis)  209 us
    ppermute x7, waiting for transfers between devices, shards(): lax.ppermute(ring[-1], 'col', [(dev, (dev + 1) % 8) for dev in range(8)])  150 us
    unnamed x1, other arithmetic  93.9 us
    psum x1, waiting for transfers between devices, shards(): totals = lax.psum(partial_value, 'row')  87.5 us
    dot_general x1, matrix products, shards(): lax.dot_general(updated, spread.reshape(brows * nb, wide), (((0,), (0,)),...  59.9 us
    reshape x1, local copies, waits for them, and re-layouts, shards(): schur = updated.reshape(brows, 1, nb, bcols, 1, nb)  48.3 us
    all_to_all x1, waiting for transfers between devices, shards(): lax.all_to_all(totals, 'col', split_axis=2, concat_axis=2, tiled=True)  42.9 us
    unnamed x21, local copies, waits for them, and re-layouts  42.8 us
  transfers between devices with their start and end apart: 11, of which 10 were waited for; matrix products, arithmetic and copies ran while one was open for 12% of the time, Pallas kernels for 0%

profile of v1, /device:TPU:0, one launch (start us, length us, event | category | flops | bytes accessed | tf_op | source)
XLA Modules:
  0.0 868.8 jit_solution(846632964294410241)
XLA Ops:
  7.2 93.9 %reduce.2 = f32[16,256,8,256]{3,2,1,0:T(8,128)} reduce(f32[16,1,256,8,1,256]{5,4,3,2,1,0:T(1,128)} %param.6, f32[]{:T(128)} %constant.98), dimensions={1,4}, to_apply=%param.6.reduce_sub_computation | reduce | bytes 67108864 | tf_op args[0]
  101.1 30.0 %copy.44 = f32[512,8,8,256]{3,1,2,0:T(8,128)} copy(f32[512,8,8,256]{3,2,1,0:T(8,128)} %bitcast.46) | data formatting | bytes 67108864
  131.1 7.7 convolution_select_fusion
  140.6 157.4 %all-reduce.5.cloned.1.call-done = f32[4096,256]{1,0:T(8,128)} async-done(((f32[4096,256]{1,0:T(8,128)}), f32[4096,256]{1,0:T(8,128)}) %all-reduce.5.cloned.1.call-update) | async-done | bytes 4194320 | tf_op jit(solution)/shard_map/psum | solution.py:11
  301.5 51.3 %all-reduce.9.cloned.1.call-done = (f32[2048,256]{1,0:T(8,128)}, f32[256,64]{0,1:T(8,128)}) async-done(((f32[2048,256]{1,0:T(8,128)}, f32[256,64]{0,1:T(8,128)}), (f32[2048,256]{1,0:T(8,128)}, f32[256,64]{0,1:T(8,128)})) %all-reduce.9.cloned.1.call-update) | async-done | bytes 2162704 | tf_op jit(solution)/shard_map/psum | solution.py:11
  354.0 6.3 convolution_subtract_fusion.1
  364.1 26.1 %collective-permute-done = f32[16,256,64]{1,2,0:T(8,128)S(1)} collective-permute-done((f32[16,256,64]{1,2,0:T(8,128)}, f32[16,256,64]{1,2,0:T(8,128)S(1)}, u32[]{:S(2)}, u32[]{:S(2)}) %collective-permute-start) | collective-permute-done | bytes 1048608 | tf_op jit(solution)/shard_map/ppermute | solution.py:48
  390.2 26.5 %collective-permute-done.1 = f32[16,256,64]{1,2,0:T(8,128)S(1)} collective-permute-done((f32[16,256,64]{1,2,0:T(8,128)S(1)}, f32[16,256,64]{1,2,0:T(8,128)S(1)}, u32[]{:S(2)}, u32[]{:S(2)}) %collective-permute-start.1) | collective-permute-done | bytes 1048608 | tf_op jit(solution)/shard_map/ppermute | solution.py:48
  417.7 25.6 %collective-permute-done.2 = f32[16,256,64]{1,2,0:T(8,128)S(1)} collective-permute-done((f32[16,256,64]{1,2,0:T(8,128)S(1)}, f32[16,256,64]{1,2,0:T(8,128)S(1)}, u32[]{:S(2)}, u32[]{:S(2)}) %collective-permute-start.2) | collective-permute-done | bytes 1048608 | tf_op jit(solution)/shard_map/ppermute | solution.py:48
  444.3 24.8 %collective-permute-done.3 = f32[16,256,64]{1,2,0:T(8,128)S(1)} collective-permute-done((f32[16,256,64]{1,2,0:T(8,128)S(1)}, f32[16,256,64]{1,2,0:T(8,128)S(1)}, u32[]{:S(2)}, u32[]{:S(2)}) %collective-permute-start.3) | collective-permute-done | bytes 1048608 | tf_op jit(solution)/shard_map/ppermute | solution.py:48
  470.1 24.0 %collective-permute-done.4 = f32[16,256,64]{1,2,0:T(8,128)} collective-permute-done((f32[16,256,64]{1,2,0:T(8,128)S(1)}, f32[16,256,64]{1,2,0:T(8,128)}, u32[]{:S(2)}, u32[]{:S(2)}) %collective-permute-start.4) | collective-permute-done | bytes 1048608 | tf_op jit(solution)/shard_map/ppermute | solution.py:48
  494.1 23.4 %collective-permute-done.5 = f32[16,256,64]{1,2,0:T(8,128)} collective-permute-done((f32[16,256,64]{1,2,0:T(8,128)}, f32[16,256,64]{1,2,0:T(8,128)}, u32[]{:S(2)}, u32[]{:S(2)}) %collective-permute-start.5) | collective-permute-done | bytes 1048608 | tf_op jit(solution)/shard_map/ppermute | solution.py:48
  517.5 34.7 %convolution_subtract_fusion = f32[4096,2048]{1,0:T(8,128)} fusion(f32[4096,2048]{1,0:T(8,128)} %bitcast.45, f32[4096,256]{1,0:T(8,128)} %all-reduce.5.cloned.1.call-done, f32[2048,256]{1,0:T(8,128)} %get-tuple-element.24), kind=kOutput, calls=%fused_computation | convolution fusion | flops 25778192384 | bytes 73400320 | tf_op jit(solution)/shard_map/dot_general | solution.py:38
  554.2 3.3 copy.28
  565.7 3.2 copy.24
  568.9 3.2 copy.23
  572.1 24.4 %concatenate.8 = f32[16,256,1024]{2,1,0:T(8,128)} concatenate(f32[16,256,64]{2,1,0:T(8,128)} %copy.23, f32[16,256,64]{2,1,0:T(8,128)} %copy.24, f32[16,256,64]{2,1,0:T(8,128)} %copy.25, f32[16,256,64]{2,1,0:T(8,128)} %copy.26, f32[16,256,64]{2,1,0:T(8,128)} %copy.27, f32[16,256,64]{2,1,0:T(8,128)} %copy.28, f32[16,256,64]{2,1,0:T(8,128)} %copy.29, ...), dimensions={2} | concatenate | bytes 33554432 | tf_op jit(solution)/shard_map/jit(_roll_dynamic)/concatenate | solution.py:49
  596.5 6.2 constant_dynamic-slice_fusion.1
  602.7 59.9 %fusion.3 = f32[2048,512]{0,1:T(8,128)S(1)} fusion(f32[4096,2048]{1,0:T(8,128)} %convolution_subtract_fusion, f32[4096,512]{1,0:T(8,128)S(1)} %bitcast.51), kind=kOutput, calls=%fused_computation.14 | convolution fusion | flops 51539607552 | bytes 46137344 | tf_op jit(solution)/shard_map/dot_general | solution.py:53
  662.6 4.0 copy.46
  666.6 87.5 %all-reduce.7.cloned.1.call-done = f32[8,256,8,64]{1,0,3,2:T(8,128)} async-done(((f32[8,256,8,64]{1,0,3,2:T(8,128)}), f32[8,256,8,64]{1,0,3,2:T(8,128)}) %all-reduce.7.cloned.1.call-update) | async-done | bytes 4194320 | tf_op jit(solution)/shard_map/psum | solution.py:60
  754.0 5.5 all-to-all-start
  759.7 48.3 %reshape.98 = f32[16,1,256,8,1,256]{5,4,3,2,1,0:T(1,128)} reshape(f32[4096,2048]{1,0:T(8,128)} %convolution_subtract_fusion) | data formatting | bytes 67108864 | tf_op jit(solution)/shard_map/reshape | solution.py:67
  809.6 42.9 %all-to-all-done = f32[8,256,8,64]{1,0,3,2:T(8,128)} async-done(((f32[8,256,8,64]{1,0,3,2:T(8,128)}), f32[8,256,8,64]{1,0,3,2:T(8,128)}, u32[]{:S(2)}, u32[]{:S(2)}) %all-to-all-start) | async-done | bytes 4194336 | tf_op jit(solution)/shard_map/all_to_all | solution.py:62
  (50 shorter events, 34.7 us)
Async XLA Ops:
  7.2 123.9 %copy-start = (f32[256,256]{1,0:T(8,128)S(1)}, f32[256,256]{1,0:T(8,128)}, u32[]{:S(2)}) copy-start(f32[256,256]{1,0:T(8,128)} %param.7) | copy-start | bytes 786436
  7.2 290.9 %all-reduce.5.cloned.1.call-start = ((), (), s32[]{:S(2)}) async-start(), calls=%async_computation.1 | async-start | bytes 8388608 | tf_op jit(solution)/shard_map/psum | solution.py:11
  138.8 1.2 copy-start.2
  138.8 214.0 %all-reduce.9.cloned.1.call-start = ((), (), s32[]{:S(2)}) async-start(), calls=%async_computation.3 | async-start | bytes 4325376 | tf_op jit(solution)/shard_map/psum | solution.py:11
  301.2 452.8 %all-reduce.7.cloned.1.call-start = ((), (), s32[]{:S(2)}) async-start(), calls=%async_computation.2 | async-start | bytes 8388608 | tf_op jit(solution)/shard_map/psum | solution.py:60
  362.7 27.6 %collective-permute-start = (f32[16,256,64]{1,2,0:T(8,128)}, f32[16,256,64]{1,2,0:T(8,128)S(1)}, u32[]{:S(2)}, u32[]{:S(2)}) collective-permute-start(f32[16,256,64]{1,2,0:T(8,128)} %copy.22), channel_id=1, source_target_pairs={{0,1},{1,2},{2,3},{3,4},{4,5},{5,6},{6,7},{7,0},{8,9},{9,10},{10,1... | collective-permute-start | bytes 3145736 | tf_op jit(solution)/shard_map/ppermute | solution.py:48
  390.2 26.5 %collective-permute-start.1 = (f32[16,256,64]{1,2,0:T(8,128)S(1)}, f32[16,256,64]{1,2,0:T(8,128)S(1)}, u32[]{:S(2)}, u32[]{:S(2)}) collective-permute-start(f32[16,256,64]{1,2,0:T(8,128)S(1)} %collective-permute-done), channel_id=1, source_target_pairs={{0,1},{1,2},{2,3},{3,4},{4,5},{5,6},{6,7},{7,0},{8,9},{9,10},{10,1... | collective-permute-start | bytes 3145736 | tf_op jit(solution)/shard_map/ppermute | solution.py:48
  416.7 1.0 copy-start.3
  417.7 25.6 %collective-permute-start.2 = (f32[16,256,64]{1,2,0:T(8,128)S(1)}, f32[16,256,64]{1,2,0:T(8,128)S(1)}, u32[]{:S(2)}, u32[]{:S(2)}) collective-permute-start(f32[16,256,64]{1,2,0:T(8,128)S(1)} %collective-permute-done.1), channel_id=1, source_target_pairs={{0,1},{1,2},{2,3},{3,4},{4,5},{5,6},{6,7},{7,0},{8,9},{9,10},{10,1... | collective-permute-start | bytes 3145736 | tf_op jit(solution)/shard_map/ppermute | solution.py:48
  443.3 1.0 copy-start.4
  444.3 24.8 %collective-permute-start.3 = (f32[16,256,64]{1,2,0:T(8,128)S(1)}, f32[16,256,64]{1,2,0:T(8,128)S(1)}, u32[]{:S(2)}, u32[]{:S(2)}) collective-permute-start(f32[16,256,64]{1,2,0:T(8,128)S(1)} %collective-permute-done.2), channel_id=1, source_target_pairs={{0,1},{1,2},{2,3},{3,4},{4,5},{5,6},{6,7},{7,0},{8,9},{9,10},{10,1... | collective-permute-start | bytes 3145736 | tf_op jit(solution)/shard_map/ppermute | solution.py:48
  469.1 1.0 copy-start.5
  470.1 24.0 %collective-permute-start.4 = (f32[16,256,64]{1,2,0:T(8,128)S(1)}, f32[16,256,64]{1,2,0:T(8,128)}, u32[]{:S(2)}, u32[]{:S(2)}) collective-permute-start(f32[16,256,64]{1,2,0:T(8,128)S(1)} %collective-permute-done.3), channel_id=1, source_target_pairs={{0,1},{1,2},{2,3},{3,4},{4,5},{5,6},{6,7},{7,0},{8,9},{9,10},{10,1... | collective-permute-start | bytes 3145736 | tf_op jit(solution)/shard_map/ppermute | solution.py:48
  494.1 23.4 %collective-permute-start.5 = (f32[16,256,64]{1,2,0:T(8,128)}, f32[16,256,64]{1,2,0:T(8,128)}, u32[]{:S(2)}, u32[]{:S(2)}) collective-permute-start(f32[16,256,64]{1,2,0:T(8,128)} %collective-permute-done.4), channel_id=1, source_target_pairs={{0,1},{1,2},{2,3},{3,4},{4,5},{5,6},{6,7},{7,0},{8,9},{9,10},{10,1... | collective-permute-start | bytes 3145736 | tf_op jit(solution)/shard_map/ppermute | solution.py:48
  517.5 51.4 %collective-permute-start.6 = (f32[16,256,64]{1,2,0:T(8,128)}, f32[16,256,64]{1,2,0:T(8,128)}, u32[]{:S(2)}, u32[]{:S(2)}) collective-permute-start(f32[16,256,64]{1,2,0:T(8,128)} %collective-permute-done.5), channel_id=1, source_target_pairs={{0,1},{1,2},{2,3},{3,4},{4,5},{5,6},{6,7},{7,0},{8,9},{9,10},{10,1... | collective-permute-start | bytes 3145736 | tf_op jit(solution)/shard_map/ppermute | solution.py:48
  554.1 6.4 copy-start.6
  666.5 93.0 %copy-start.7 = (f32[4]{0:T(128)S(1)}, f32[4]{0:T(128)}, u32[]{:S(2)}) copy-start(f32[4]{0:T(128)} %param.9) | copy-start | bytes 52
  754.0 98.5 %all-to-all-start = ((f32[8,256,8,64]{1,0,3,2:T(8,128)}), f32[8,256,8,64]{1,0,3,2:T(8,128)}, u32[]{:S(2)}, u32[]{:S(2)}) async-start(f32[8,256,8,64]{1,0,3,2:T(8,128)} %all-reduce.7.cloned.1.call-done), calls=%async_computation | async-start | bytes 8388608 | tf_op jit(solution)/shard_map/all_to_all | solution.py:62
  853.8 8.3 copy-start.1
Sparse Core Ops, SparseCore 0:
  138.9 159.1 all-reduce.4
  301.3 51.4 all-reduce.8
  666.7 87.3 all-reduce.6
